TPU v7x, 256 devices: a whole 4x4x8 slice. The times are simulated.
256 devices in a mesh: seq: 4 (over z_hi), expert: 64 (over z_lo, y, x, core).
Axes of the slice: x: 4, y: 4, z: 8 (z_hi: 4, z_lo: 2; z = z_hi * 2 + z_lo), core: 2. Of those that a mesh axis runs over, the one named last changes fastest.
Arguments:
- tokens: bfloat16 [32768, 4096], P(('seq', 'expert')), may hold values from -6 to 6
- expert_ids: int32 [32768, 1], P(('seq', 'expert')), may hold values from 0 to 63; in each aligned block of 128 rows (0 to 127, 128 to 255, ...) at most 3 rows name the same one
- gate_weights: bfloat16 [32768, 1], P(('seq', 'expert')), may hold values from 0.049804688 to 1
- w_gate: bfloat16 [64, 768, 4096], P('expert', 'seq'), may hold values from -0.09375 to 0.09375
- w_up: bfloat16 [64, 768, 4096], P('expert', 'seq'), may hold values from -0.09375 to 0.09375
- w_down: bfloat16 [64, 768, 4096], P('expert', 'seq'), may hold values from -0.21875 to 0.21875
- cotangent: bfloat16 [32768, 4096], P(('seq', 'expert')), may hold values from -2 to 2
Outputs:
- d_tokens: bfloat16 [32768, 4096], P(('seq', 'expert'))
- d_gates: float32 [32768, 1], P(('seq', 'expert'))
- grad_gate: bfloat16 [64, 768, 4096], P('expert', 'seq')
- grad_up: bfloat16 [64, 768, 4096], P('expert', 'seq')
- grad_down: bfloat16 [64, 768, 4096], P('expert', 'seq')
Inputs may be any that keep to these rules, and one draw needn't show every extreme that they name: `expert_ids`: each row names one expert. Among the rows of one device (aligned blocks of 128 rows) no expert is named more than 3 times, and in every draw some expert is named exactly 3 times in some block.
All inputs are finite; a program needn't handle non-finite values.
Results may differ from a plain program's by a relative error of at most 0.012.
Values may be sent and summed in bfloat16 or wider, within the bound.
No kernel may reach another device: no remote copies, remote signals or barrier semaphores. Data moves between devices by JAX's collectives and lax.ppermute only.
A program may use at most 192 MiB of HBM per device.

v0:
```python
import jax
import jax.numpy as jnp
import numpy as np
from jax import lax
from jax.sharding import Mesh, PartitionSpec as P

CAP = 3
ZLO = 2
LANES = 128
COLUMN = ("seq", "zlo")
PLANE = ("y", "x", "core")
EXPERT = ("zlo", "y", "x", "core")
BF = jnp.bfloat16
F32 = jnp.float32


def dot(a, b, out=F32):
    return lax.dot_general(a, b, (((1,), (0,)), ((), ())), preferred_element_type=out)


def dot_t(a, b, out=F32):
    return lax.dot_general(a, b, (((1,), (1,)), ((), ())), preferred_element_type=out)


def tdot(a, b, out=F32):
    return lax.dot_general(a, b, (((0,), (0,)), ((), ())), preferred_element_type=out)


def column_gather(values, depth, me):
    got = [values]
    for far in range(1, depth):
        got.append(lax.ppermute(values, COLUMN, [(i, (i + far) % depth) for i in range(depth)]))
    picked = lax.rem(me - lax.iota(jnp.int32, depth) + depth, depth)
    return jnp.take(jnp.stack(got), picked, axis=0)


def per_device(tokens, expert_ids, gate_weights, w_gate, w_up, w_down, cotangent):
    groups = lax.axis_size("seq")
    plane = lax.axis_size(PLANE)
    depth = groups * ZLO
    experts = plane * ZLO
    rows, width = tokens.shape
    half = width // 2
    send = experts * CAP
    held = send * groups
    block = depth * CAP
    zlo = lax.axis_index("zlo")
    me = lax.axis_index("seq") * ZLO + zlo
    wg, wu, wd = (w_gate[0], w_up[0], w_down[0])
    ids = expert_ids[:, 0]
    here = lax.iota(jnp.int32, rows)
    same = (ids[:, None] == ids[None, :]) & (here[None, :] < here[:, None])
    rank = jnp.sum(same.astype(jnp.int32), axis=1)
    slot = ids * CAP + rank
    to_slot = (slot[None, :] == lax.iota(jnp.int32, send)[:, None]).astype(BF)
    from_slot = (slot[:, None] == lax.iota(jnp.int32, send)[None, :]).astype(BF)
    x_column = lax.all_gather(tokens, COLUMN, axis=0, tiled=True)
    dy_send = dot(to_slot, cotangent, BF).reshape(experts, CAP, width)
    dy_mine = lax.all_to_all(dy_send, EXPERT, 0, 0, tiled=True).reshape(send, width)
    dy_held = lax.all_gather(dy_mine, "seq", axis=0, tiled=True)
    code = ids % plane * block + me * CAP + rank + held * (ids // plane)
    meta = jnp.stack([code.astype(F32), gate_weights[:, 0].astype(F32)])
    meta = column_gather(meta, depth, me)
    target = meta[:, 0, :].reshape(-1).astype(jnp.int32) - held * zlo
    gates_column = meta[:, 1, :].reshape(-1)
    in_column = depth * rows
    hit = target[None, :] == lax.iota(jnp.int32, held)[:, None]
    pick = hit.astype(BF)
    unpick = (target[:, None] == lax.iota(jnp.int32, held)[None, :]).astype(BF)
    gate_send = jnp.sum(jnp.where(hit, gates_column[None, :], 0.0), axis=1).reshape(plane, block)
    gate_x = lax.all_to_all(gate_send, PLANE, 0, 0, tiled=True).reshape(held)
    x_send = dot(pick, x_column, BF).reshape(plane, block, width)
    x_held = lax.all_to_all(x_send, PLANE, 0, 0, tiled=True).reshape(held, width)
    at = lax.iota(jnp.int32, held)
    as_x = at % (plane * CAP) // CAP * block + at // (plane * CAP) * CAP + at % CAP
    turn = as_x[:, None] == at[None, :]
    turn_bf = turn.astype(BF)
    turn_f32 = turn.astype(F32)
    pre_x = jnp.concatenate([dot_t(x_held, wg), dot_t(x_held, wu)], axis=1)
    pre = lax.dot_general(
        turn_f32,
        pre_x,
        (((1,), (0,)), ((), ())),
        precision=lax.Precision.HIGHEST,
        preferred_element_type=F32,
    )
    hidden = wg.shape[0]
    pre_gate, pre_up = (pre[:, :hidden], pre[:, hidden:])
    gate_col = jnp.sum(jnp.where(turn, gate_x[None, :], 0.0), axis=1)[:, None]
    back = dot_t(dy_held, wd)
    sigmoid_gate = jax.nn.sigmoid(pre_gate)
    silu_gate = pre_gate * sigmoid_gate
    activated = silu_gate * pre_up
    route = jnp.sum(activated * back, axis=1, keepdims=True).astype(BF)
    scaled = (gate_col * activated).astype(BF)
    gated_back = gate_col * back
    g_gate = (gated_back * pre_up * sigmoid_gate * (1.0 + pre_gate * (1.0 - sigmoid_gate))).astype(
        BF
    )
    g_up = (gated_back * silu_gate).astype(BF)
    part_a = (dot(g_gate, wg[:, :half]) + dot(g_up, wu[:, :half])).astype(BF)
    sum_a = lax.psum_scatter(part_a, "seq", scatter_dimension=0, tiled=True)
    g_gate_x = tdot(turn_bf, g_gate, BF)
    g_up_x = tdot(turn_bf, g_up, BF)
    route_x = tdot(turn_bf, jnp.broadcast_to(route, (held, LANES)), BF)
    part_b = (dot(g_gate_x, wg[:, half:]) + dot(g_up_x, wu[:, half:])).astype(BF)
    part_b = jnp.concatenate([part_b, route_x], axis=1)
    back_b = lax.all_to_all(part_b.reshape(plane, block, half + LANES), PLANE, 0, 0, tiled=True)
    column_b = dot(unpick, back_b.reshape(held, half + LANES), BF)
    sum_b = lax.psum_scatter(column_b, COLUMN, scatter_dimension=0, tiled=True)
    back_a = lax.all_to_all(sum_a.reshape(experts, CAP, half), EXPERT, 0, 0, tiled=True)
    rows_a = dot(from_slot, back_a.reshape(send, half), BF)
    grad_gate = tdot(g_gate_x, x_held, BF)
    grad_up = tdot(g_up_x, x_held, BF)
    grad_down = tdot(scaled, dy_held, BF)
    d_tokens = jnp.concatenate([rows_a, sum_b[:, :half]], axis=1)
    d_gates = sum_b[:, half : half + 1].astype(F32)
    return (d_tokens, d_gates, grad_gate[None], grad_up[None], grad_down[None])


def solution(mesh):
    groups, experts = (mesh.shape["seq"], mesh.shape["expert"])
    side = int(np.sqrt(experts // (2 * ZLO)))
    fine = Mesh(
        np.asarray(mesh.devices).reshape(groups, ZLO, experts // (2 * ZLO * side), side, 2),
        ("seq", "zlo", "y", "x", "core"),
    )
    by_row = P(("seq",) + EXPERT, None)
    by_expert = P(EXPERT, "seq", None)
    return jax.shard_map(
        per_device,
        mesh=fine,
        in_specs=(by_row, by_row, by_row, by_expert, by_expert, by_expert, by_row),
        out_specs=(by_row, by_row, by_expert, by_expert, by_expert),
        check_vma=False,
    )
```

profile of v0, /device:TPU:1, one launch (start us, length us, event | category | flops | bytes accessed | tf_op | source)
XLA Modules:
  0.0 406.8 jit_solution(1096296496318085417)
XLA Ops:
  13.6 10.5 %all-to-all-start.1 = ((bf16[64,3,4096]{2,1,0:T(4,128)(2,1)}), bf16[64,3,4096]{2,1,0:T(4,128)(2,1)}, u32[]{:S(2)}, u32[]{:S(2)}) async-start(bf16[64,3,4096]{2,1,0:T(4,128)(2,1)} %reshape.278), calls=%async_computation.1 | async-start | bytes 4194304 | tf_op jit(solution)/shard_map/all_to_all | solution.py:59
  24.3 5.2 %collective-permute-start.5 = (f32[2,128]{1,0:T(2,128)S(1)}, f32[2,128]{1,0:T(2,128)S(1)}, u32[]{:S(2)}, u32[]{:S(2)}) collective-permute-start(f32[2,128]{1,0:T(2,128)S(1)} %pad_maximum_fusion.2), channel_id=1, source_target_pairs={{0,192},{32,224},{64,0},{96,32},{128,64},{160,96},{192,128},{224,1... | collective-permute-start | bytes 3080 | tf_op jit(solution)/shard_map/ppermute | solution.py:32
  30.9 4.2 %collective-permute-start.3 = (f32[2,128]{1,0:T(2,128)S(1)}, f32[2,128]{1,0:T(2,128)S(1)}, u32[]{:S(2)}, u32[]{:S(2)}) collective-permute-start(f32[2,128]{1,0:T(2,128)S(1)} %pad_maximum_fusion.2), channel_id=1, source_target_pairs={{0,128},{32,160},{64,192},{96,224},{128,0},{160,32},{192,64},{224,... | collective-permute-start | bytes 3080 | tf_op jit(solution)/shard_map/ppermute | solution.py:32
  36.7 31.4 %collective-permute-done = f32[2,128]{1,0:T(2,128)S(1)} collective-permute-done((f32[2,128]{1,0:T(2,128)S(1)}, f32[2,128]{1,0:T(2,128)S(1)}, u32[]{:S(2)}, u32[]{:S(2)}) %collective-permute-start) | collective-permute-done | bytes 1056 | tf_op jit(solution)/shard_map/ppermute | solution.py:32
  68.0 4.3 %collective-permute-start.1 = (f32[2,128]{1,0:T(2,128)S(1)}, f32[2,128]{1,0:T(2,128)S(1)}, u32[]{:S(2)}, u32[]{:S(2)}) collective-permute-start(f32[2,128]{1,0:T(2,128)S(1)} %pad_maximum_fusion.2), channel_id=1, source_target_pairs={{0,64},{32,96},{64,128},{96,160},{128,192},{160,224},{192,0},{224,... | collective-permute-start | bytes 3080 | tf_op jit(solution)/shard_map/ppermute | solution.py:32
  75.3 3.6 collective-permute-start.6
  80.2 4.3 %reshape.279 = bf16[192,4096]{1,0:T(8,128)(2,1)} reshape(bf16[64,3,4096]{2,1,0:T(4,128)(2,1)} %all-to-all-done.1) | data formatting | bytes 3145728 | tf_op jit(solution)/shard_map/reshape | solution.py:59
  85.6 9.5 %all-to-all-start = ((f32[32,1,24]{2,1,0:T(1,128)}), f32[32,1,24]{2,1,0:T(1,128)S(1)}, u32[]{:S(2)}, u32[]{:S(2)}) async-start(f32[32,1,24]{2,1,0:T(1,128)} %bitcast.17), calls=%async_computation | async-start | bytes 32768 | tf_op jit(solution)/shard_map/all_to_all | solution.py:71
  95.2 33.2 %all-gather.5.cloned.1.call-done = bf16[1024,4096]{1,0:T(8,128)(2,1)} async-done(((bf16[128,4096]{1,0:T(8,128)(2,1)}), bf16[1024,4096]{1,0:T(8,128)(2,1)}) %all-gather.5.cloned.1.call-update) | async-done | bytes 8388624 | tf_op jit(solution)/shard_map/all_gather | solution.py:57
  128.4 11.8 %fusion = bf16[768,4096]{1,0:T(8,128)(2,1)} fusion(bf16[1024,4096]{1,0:T(8,128)(2,1)} %all-gather.5.cloned.1.call-done, s32[1024]{0:T(1024)S(1)} %bitcast.98), kind=kOutput, calls=%fused_computation.10 | convolution fusion | flops 6443237376 | bytes 14684160 | tf_op jit(solution)/shard_map/dot_general | solution.py:18
  140.2 7.6 %all-to-all-start.2 = ((bf16[32,24,4096]{2,1,0:T(8,128)(2,1)}), bf16[32,24,4096]{2,1,0:T(8,128)(2,1)}, u32[]{:S(2)}, u32[]{:S(2)}) async-start(bf16[32,24,4096]{2,1,0:T(8,128)(2,1)} %bitcast.91), calls=%async_computation.2 | async-start | bytes 12582912 | tf_op jit(solution)/shard_map/all_to_all | solution.py:73
  149.7 71.1 %all-to-all-done.2 = bf16[32,24,4096]{2,1,0:T(8,128)(2,1)} async-done(((bf16[32,24,4096]{2,1,0:T(8,128)(2,1)}), bf16[32,24,4096]{2,1,0:T(8,128)(2,1)}, u32[]{:S(2)}, u32[]{:S(2)}) %all-to-all-start.2) | async-done | bytes 6291488 | tf_op jit(solution)/shard_map/all_to_all | solution.py:73
  220.8 5.6 %fusion.64 = f32[768,192]{0,1:T(8,128)S(1)} fusion(bf16[768,4096]{1,0:T(8,128)(2,1)} %bitcast.20, bf16[1,192,4096]{2,1,0:T(8,128)(2,1)} %param.11), kind=kOutput, calls=%fused_computation.122 | convolution fusion | flops 1207959552 | bytes 8454144 | tf_op jit(solution)/shard_map/dot_general | solution.py:22
  226.4 5.0 %fusion.66 = f32[768,192]{0,1:T(8,128)S(1)} fusion(bf16[768,4096]{1,0:T(8,128)(2,1)} %bitcast.20, bf16[1,192,4096]{2,1,0:T(8,128)(2,1)S(1)} %copy-done.2), kind=kOutput, calls=%fused_computation.124 | convolution fusion | flops 1207959552 | bytes 8454144 | tf_op jit(solution)/shard_map/dot_general | solution.py:22
  234.3 11.2 %all-gather.3.cloned.1.call-done = bf16[768,4096]{1,0:T(8,128)(2,1)} async-done(((bf16[192,4096]{1,0:T(8,128)(2,1)}), bf16[768,4096]{1,0:T(8,128)(2,1)}) %all-gather.3.cloned.1.call-update) | async-done | bytes 6291472 | tf_op jit(solution)/shard_map/all_gather | solution.py:60
  245.5 5.4 %multiply_convert_fusion.1 = (bf16[768,192]{0,1:T(8,128)(2,1)S(1)}, bf16[768,192]{0,1:T(8,128)(2,1)S(1)}, bf16[768]{0:T(1024)(128)(2,1)S(1)}) fusion(f32[768]{0:T(1024)S(1)} %select_reduce_fusion.1, f32[768,384]{0,1:T(8,128)} %fusion.5, bf16[768,4096]{1,0:T(8,128)(2,1)} %all-gather.3.cloned.1.call-done, bf16[1,192,4096]{2,1,0:T(8,128)(2,1)S(1)} %copy-done), kind=kOutput, calls=%fused_computation.38 | convolution fusion | flops 1210465536 | bytes 9638400 | tf_op jit(solution)/shard_map/dot_general | solution.py:22
  261.3 55.3 %all_to_all.29 = bf16[32,24,2176]{2,1,0:T(8,128)(2,1)S(1)} all-to-all(bf16[32,24,2176]{2,1,0:T(8,128)(2,1)S(1)} %bitcast.90), channel_id=1, replica_groups=mesh['seq'=4,'zlo'=2,'y'=4,'x'=4,'core'=2] {'y','x','core'}, dimensions={0} | all-to-all | bytes 6684672 | tf_op jit(solution)/shard_map/all_to_all | solution.py:108
  316.6 5.7 %fusion.1 = bf16[1024,2176]{1,0:T(8,128)(2,1)} fusion(bf16[768,2176]{1,0:T(8,128)(2,1)S(1)} %bitcast.92, s32[1024]{0:T(1024)S(1)} %bitcast.99), kind=kOutput, calls=%fused_computation.11 | convolution fusion | flops 3423338496 | bytes 7802880 | tf_op jit(solution)/shard_map/dot_general | solution.py:18
  322.3 6.4 %reduce-scatter.3.cloned.1.call-done = bf16[192,2048]{1,0:T(8,128)(2,1)} async-done(((bf16[768,2048]{1,0:T(8,128)(2,1)}), bf16[192,2048]{1,0:T(8,128)(2,1)}) %reduce-scatter.3.cloned.1.call-update) | async-done | bytes 786448 | tf_op jit(solution)/shard_map/reduce_scatter | solution.py:102
  332.0 8.1 %all-to-all-start.3 = ((bf16[64,3,2048]{2,1,0:T(4,128)(2,1)}), bf16[64,3,2048]{2,1,0:T(4,128)(2,1)S(1)}, u32[]{:S(2)}, u32[]{:S(2)}) async-start(bf16[64,3,2048]{2,1,0:T(4,128)(2,1)} %reshape.282), calls=%async_computation.4 | async-start | bytes 2097152 | tf_op jit(solution)/shard_map/all_to_all | solution.py:111
  340.1 5.8 %convolution_bitcast_fusion.2 = bf16[1,192,4096]{2,1,0:T(8,128)(2,1)} fusion(bf16[768,192]{0,1:T(8,128)(2,1)S(1)} %fusion.4, bf16[768,4096]{1,0:T(8,128)(2,1)} %bitcast.20), kind=kOutput, calls=%fused_computation.5 | convolution fusion | flops 1207959552 | bytes 8159232 | tf_op jit(solution)/shard_map/dot_general | solution.py:26
  345.9 5.5 %convolution_bitcast_fusion.1 = bf16[1,192,4096]{2,1,0:T(8,128)(2,1)} fusion(bf16[768,192]{0,1:T(8,128)(2,1)S(1)} %copy-done.6, bf16[768,4096]{1,0:T(8,128)(2,1)} %bitcast.20), kind=kOutput, calls=%fused_computation.4 | convolution fusion | flops 1207959552 | bytes 8159232 | tf_op jit(solution)/shard_map/dot_general | solution.py:26
  354.1 13.2 %all-to-all-done.3 = bf16[64,3,2048]{2,1,0:T(4,128)(2,1)S(1)} async-done(((bf16[64,3,2048]{2,1,0:T(4,128)(2,1)}), bf16[64,3,2048]{2,1,0:T(4,128)(2,1)S(1)}, u32[]{:S(2)}, u32[]{:S(2)}) %all-to-all-start.3) | async-done | bytes 786464 | tf_op jit(solution)/shard_map/all_to_all | solution.py:111
  368.4 28.3 %reduce-scatter.5.cloned.1.call-done = bf16[128,2176]{1,0:T(8,128)(2,1)} async-done(((bf16[1024,2176]{1,0:T(8,128)(2,1)}), bf16[128,2176]{1,0:T(8,128)(2,1)}) %reduce-scatter.5.cloned.1.call-update) | async-done | bytes 557072 | tf_op jit(solution)/shard_map/reduce_scatter | solution.py:110
  (91 shorter events, 40.3 us)
Async XLA Ops:
  7.2 238.4 %copy-start = (bf16[1,192,4096]{2,1,0:T(8,128)(2,1)S(1)}, bf16[1,192,4096]{2,1,0:T(8,128)(2,1)}, u32[]{:S(2)}) copy-start(bf16[1,192,4096]{2,1,0:T(8,128)(2,1)} %param.12) | copy-start | bytes 4718596
  7.2 121.2 %all-gather.5.cloned.1.call-start = ((), (), s32[]{:S(2)}) async-start(), calls=%async_computation.8 | async-start | bytes 9437184 | tf_op jit(solution)/shard_map/all_gather | solution.py:57
  11.3 12.9 %copy-start.8 = (bf16[128,1]{0,1:T(2,128)(2,1)S(1)}, bf16[128,1]{0,1:T(2,128)(2,1)}, u32[]{:S(2)}) copy-start(bf16[128,1]{0,1:T(2,128)(2,1)} %param.9) | copy-start | bytes 772
  11.3 12.9 %copy-start.7 = (s32[128,1]{0,1:T(1,128)S(1)}, s32[128,1]{0,1:T(1,128)}, u32[]{:S(2)}) copy-start(s32[128,1]{0,1:T(1,128)} %param.8) | copy-start | bytes 1540
  13.6 66.5 %all-to-all-start.1 = ((bf16[64,3,4096]{2,1,0:T(4,128)(2,1)}), bf16[64,3,4096]{2,1,0:T(4,128)(2,1)}, u32[]{:S(2)}, u32[]{:S(2)}) async-start(bf16[64,3,4096]{2,1,0:T(4,128)(2,1)} %reshape.278), calls=%async_computation.1 | async-start | bytes 4194304 | tf_op jit(solution)/shard_map/all_to_all | solution.py:59
  24.2 221.4 %all-gather.3.cloned.1.call-start = ((), (), s32[]{:S(2)}) async-start(), calls=%async_computation.7 | async-start | bytes 7864320 | tf_op jit(solution)/shard_map/all_gather | solution.py:60
  24.3 54.6 %collective-permute-start.5 = (f32[2,128]{1,0:T(2,128)S(1)}, f32[2,128]{1,0:T(2,128)S(1)}, u32[]{:S(2)}, u32[]{:S(2)}) collective-permute-start(f32[2,128]{1,0:T(2,128)S(1)} %pad_maximum_fusion.2), channel_id=1, source_target_pairs={{0,192},{32,224},{64,0},{96,32},{128,64},{160,96},{192,128},{224,1... | collective-permute-start | bytes 3080 | tf_op jit(solution)/shard_map/ppermute | solution.py:32
  29.5 49.4 %collective-permute-start.4 = (f32[2,128]{1,0:T(2,128)S(1)}, f32[2,128]{1,0:T(2,128)S(1)}, u32[]{:S(2)}, u32[]{:S(2)}) collective-permute-start(f32[2,128]{1,0:T(2,128)S(1)} %pad_maximum_fusion.2), channel_id=1, source_target_pairs={{0,160},{32,192},{64,224},{96,0},{128,32},{160,64},{192,96},{224,1... | collective-permute-start | bytes 3080 | tf_op jit(solution)/shard_map/ppermute | solution.py:32
  30.9 47.9 %collective-permute-start.3 = (f32[2,128]{1,0:T(2,128)S(1)}, f32[2,128]{1,0:T(2,128)S(1)}, u32[]{:S(2)}, u32[]{:S(2)}) collective-permute-start(f32[2,128]{1,0:T(2,128)S(1)} %pad_maximum_fusion.2), channel_id=1, source_target_pairs={{0,128},{32,160},{64,192},{96,224},{128,0},{160,32},{192,64},{224,... | collective-permute-start | bytes 3080 | tf_op jit(solution)/shard_map/ppermute | solution.py:32
  35.2 43.7 %collective-permute-start.2 = (f32[2,128]{1,0:T(2,128)S(1)}, f32[2,128]{1,0:T(2,128)S(1)}, u32[]{:S(2)}, u32[]{:S(2)}) collective-permute-start(f32[2,128]{1,0:T(2,128)S(1)} %pad_maximum_fusion.2), channel_id=1, source_target_pairs={{0,96},{32,128},{64,160},{96,192},{128,224},{160,0},{192,32},{224,... | collective-permute-start | bytes 3080 | tf_op jit(solution)/shard_map/ppermute | solution.py:32
  35.2 32.9 %collective-permute-start = (f32[2,128]{1,0:T(2,128)S(1)}, f32[2,128]{1,0:T(2,128)S(1)}, u32[]{:S(2)}, u32[]{:S(2)}) collective-permute-start(f32[2,128]{1,0:T(2,128)S(1)} %pad_maximum_fusion.2), channel_id=1, source_target_pairs={{0,32},{32,64},{64,96},{96,128},{128,160},{160,192},{192,224},{224... | collective-permute-start | bytes 3080 | tf_op jit(solution)/shard_map/ppermute | solution.py:32
  68.0 7.2 %collective-permute-start.1 = (f32[2,128]{1,0:T(2,128)S(1)}, f32[2,128]{1,0:T(2,128)S(1)}, u32[]{:S(2)}, u32[]{:S(2)}) collective-permute-start(f32[2,128]{1,0:T(2,128)S(1)} %pad_maximum_fusion.2), channel_id=1, source_target_pairs={{0,64},{32,96},{64,128},{96,160},{128,192},{160,224},{192,0},{224,... | collective-permute-start | bytes 3080 | tf_op jit(solution)/shard_map/ppermute | solution.py:32
  75.3 4.3 %collective-permute-start.6 = (f32[2,128]{1,0:T(2,128)S(1)}, f32[2,128]{1,0:T(2,128)S(1)}, u32[]{:S(2)}, u32[]{:S(2)}) collective-permute-start(f32[2,128]{1,0:T(2,128)S(1)} %pad_maximum_fusion.2), channel_id=1, source_target_pairs={{0,224},{32,0},{64,32},{96,64},{128,96},{160,128},{192,160},{224,1... | collective-permute-start | bytes 3080 | tf_op jit(solution)/shard_map/ppermute | solution.py:32
  85.6 54.6 %all-to-all-start = ((f32[32,1,24]{2,1,0:T(1,128)}), f32[32,1,24]{2,1,0:T(1,128)S(1)}, u32[]{:S(2)}, u32[]{:S(2)}) async-start(f32[32,1,24]{2,1,0:T(1,128)} %bitcast.17), calls=%async_computation | async-start | bytes 32768 | tf_op jit(solution)/shard_map/all_to_all | solution.py:71
  140.2 80.6 %all-to-all-start.2 = ((bf16[32,24,4096]{2,1,0:T(8,128)(2,1)}), bf16[32,24,4096]{2,1,0:T(8,128)(2,1)}, u32[]{:S(2)}, u32[]{:S(2)}) async-start(bf16[32,24,4096]{2,1,0:T(8,128)(2,1)} %bitcast.91), calls=%async_computation.2 | async-start | bytes 12582912 | tf_op jit(solution)/shard_map/all_to_all | solution.py:73
  147.8 180.9 %reduce-scatter.3.cloned.1.call-start = ((), (), s32[]{:S(2)}) async-start(), calls=%async_computation.9 | async-start | bytes 3932160 | tf_op jit(solution)/shard_map/reduce_scatter | solution.py:102
  220.8 5.6 %copy-start.2 = (bf16[1,192,4096]{2,1,0:T(8,128)(2,1)S(1)}, bf16[1,192,4096]{2,1,0:T(8,128)(2,1)}, u32[]{:S(2)}) copy-start(bf16[1,192,4096]{2,1,0:T(8,128)(2,1)} %param.10) | copy-start | bytes 4718596
  255.2 141.5 %reduce-scatter.5.cloned.1.call-start = ((), (), s32[]{:S(2)}) async-start(), calls=%async_computation.10 | async-start | bytes 5013504 | tf_op jit(solution)/shard_map/reduce_scatter | solution.py:110
  332.0 35.4 %all-to-all-start.3 = ((bf16[64,3,2048]{2,1,0:T(4,128)(2,1)}), bf16[64,3,2048]{2,1,0:T(4,128)(2,1)S(1)}, u32[]{:S(2)}, u32[]{:S(2)}) async-start(bf16[64,3,2048]{2,1,0:T(4,128)(2,1)} %reshape.282), calls=%async_computation.4 | async-start | bytes 2097152 | tf_op jit(solution)/shard_map/all_to_all | solution.py:111
  340.1 5.9 %copy-start.6 = (bf16[768,192]{0,1:T(8,128)(2,1)S(1)}, bf16[768,192]{0,1:T(8,128)(2,1)}, u32[]{:S(2)}) copy-start(bf16[768,192]{0,1:T(8,128)(2,1)} %copy-done.5) | copy-start | bytes 884740
  340.1 11.4 %slice-start = ((s8[6291456]{0:T(1024)(128)(4,1)}), s8[4194304]{0:T(1024)(128)(4,1)S(1)}, s32[]{:S(2)}) async-start(s8[6291456]{0:T(1024)(128)(4,1)} %bitcast.102), calls=%async_computation.11 | async-start | bytes 8388608
  345.9 5.5 %slice-start.1 = ((s8[6291456]{0:T(1024)(128)(4,1)}), s8[2097152]{0:T(1024)(128)(4,1)S(1)}, s32[]{:S(2)}) async-start(s8[6291456]{0:T(1024)(128)(4,1)} %bitcast.102), calls=%async_computation.12 | async-start | bytes 4194304
  345.9 5.5 %copy-start.9 = (f32[768,384]{0,1:T(8,128)S(1)}, f32[768,384]{0,1:T(8,128)}, u32[]{:S(2)}) copy-start(f32[768,384]{0,1:T(8,128)} %fusion.5) | copy-start | bytes 3538948
  351.5 48.8 %copy-start.1 = (bf16[1,192,4096]{2,1,0:T(8,128)(2,1)S(1)}, bf16[1,192,4096]{2,1,0:T(8,128)(2,1)}, u32[]{:S(2)}) copy-start(bf16[1,192,4096]{2,1,0:T(8,128)(2,1)} %param.12) | copy-start | bytes 4718596
  (3 other events, 5.3 us)
Sparse Core Ops, SparseCore 0:
  9.8 118.5 all-gather.4
  130.7 114.7 all-gather.2
  255.4 73.2 reduce-scatter.2
  331.1 65.5 reduce-scatter.4
where the time goes:
time: 408 us; the launch traced here: 407 us
  waiting for transfers between devices  199 us (49%)
  matrix products  61.8 us (15%)
  starting transfers between devices  56.3 us (14%)
  blocking collectives  55.3 us (14%)
  local copies, waits for them, and re-layouts  14.7 us (4%)
  between operations  14.2 us (3%)
  other arithmetic  5.4 us (1%)
    all_to_all x1, waiting for transfers between devices, per_device(): lax.all_to_all(x_send, PLANE, 0, 0, tiled=True).reshape(held, width)  71.1 us
    all_to_all x1, blocking collectives, per_device(): lax.all_to_all(part_b.reshape(plane, block, half + LANES), PLANE, 0, 0, t...  55.3 us
    ppermute x7, waiting for transfers between devices, column_gather(): lax.ppermute(values, COLUMN, [(i, (i + far) % depth) for i in range(depth)])  34.9 us
    all_gather x1, waiting for transfers between devices, per_device(): x_column = lax.all_gather(tokens, COLUMN, axis=0, tiled=True)  33.2 us
    reduce_scatter x1, waiting for transfers between devices, per_device(): sum_b = lax.psum_scatter(column_b, COLUMN, scatter_dimension=0, tiled=True)  28.3 us
    dot_general x8, matrix products, dot(): lax.dot_general(a, b, (((1,), (0,)), ((), ())), preferred_element_type=out)  25.4 us
    ppermute x7, starting transfers between devices, column_gather(): lax.ppermute(values, COLUMN, [(i, (i + far) % depth) for i in range(depth)])  20.2 us
    dot_general x6, matrix products, tdot(): lax.dot_general(a, b, (((0,), (0,)), ((), ())), preferred_element_type=out)  17.4 us
  transfers between devices with their start and end apart: 15, of which 9 were waited for; matrix products, arithmetic and copies ran while one was open for 17% of the time, Pallas kernels for 0%

commit v1 on v0

--- a/solution.py
+++ b/solution.py
@@ -54,7 +54,9 @@
     slot = ids * CAP + rank
     to_slot = (slot[None, :] == lax.iota(jnp.int32, send)[:, None]).astype(BF)
     from_slot = (slot[:, None] == lax.iota(jnp.int32, send)[None, :]).astype(BF)
-    x_column = lax.all_gather(tokens, COLUMN, axis=0, tiled=True)
+    x_column = jnp.concatenate(
+        lax.all_to_all(jnp.stack([tokens] * lax.axis_size(COLUMN)), COLUMN, 0, 0), axis=0
+    )
     dy_send = dot(to_slot, cotangent, BF).reshape(experts, CAP, width)
     dy_mine = lax.all_to_all(dy_send, EXPERT, 0, 0, tiled=True).reshape(send, width)
     dy_held = lax.all_gather(dy_mine, "seq", axis=0, tiled=True)

time: 408 us -> 535 us (1.31)
  waiting for transfers between devices: 199 us -> 294 us
  blocking collectives: 55.3 us -> 93.2 us
  starting transfers between devices: 56.3 us -> 45.7 us
    ppermute x7, waiting for transfers between devices: 34.9 us -> 175 us  [column_gather(): lax.ppermute(values, COLUMN, [(i, (i + far) % depth) for i in range(depth)])]
    all_to_all x0 -> x1, blocking collectives: none -> 38.2 us  [per_device(): lax.all_to_all(dy_send, EXPERT, 0, 0, tiled=True).reshape(send, width)]
    all_gather x1 -> x0, waiting for transfers between devices: 33.2 us -> none  [per_device(): x_column = lax.all_gather(tokens, COLUMN, axis=0, tiled=True)]
    all_gather x1, waiting for transfers between devices: 11.2 us -> 0.91 us  [per_device(): dy_held = lax.all_gather(dy_mine, 'seq', axis=0, tiled=True)]
    ppermute x7, starting transfers between devices: 20.2 us -> 14.1 us  [column_gather(): lax.ppermute(values, COLUMN, [(i, (i + far) % depth) for i in range(depth)])]
  transfers between devices with their start and end apart: 15 -> 14, of which waited for: 9 -> 8; matrix products, arithmetic and copies ran while one was open for 17% -> 12% of each run, Pallas kernels for 0% -> 0%
where the time goes in v1:
time: 535 us; the launch traced here: 534 us
  waiting for transfers between devices  294 us (55%)
  blocking collectives  93.2 us (17%)
  matrix products  62.1 us (12%)
  starting transfers between devices  45.7 us (9%)
  local copies, waits for them, and re-layouts  19.4 us (4%)
  between operations  14.1 us (3%)
  other arithmetic  5.47 us (1%)
    ppermute x7, waiting for transfers between devices, column_gather(): lax.ppermute(values, COLUMN, [(i, (i + far) % depth) for i in range(depth)])  175 us
    all_to_all x1, waiting for transfers between devices, per_device(): lax.all_to_all(x_send, PLANE, 0, 0, tiled=True).reshape(held, width)  71.1 us
    all_to_all x1, blocking collectives, per_device(): lax.all_to_all(part_b.reshape(plane, block, half + LANES), PLANE, 0, 0, t...  55.1 us
    all_to_all x1, blocking collectives, per_device(): lax.all_to_all(dy_send, EXPERT, 0, 0, tiled=True).reshape(send, width)  38.2 us
    reduce_scatter x1, waiting for transfers between devices, per_device(): sum_b = lax.psum_scatter(column_b, COLUMN, scatter_dimension=0, tiled=True)  28.3 us
    dot_general x8, matrix products, dot(): lax.dot_general(a, b, (((1,), (0,)), ((), ())), preferred_element_type=out)  25.8 us
    dot_general x6, matrix products, tdot(): lax.dot_general(a, b, (((0,), (0,)), ((), ())), preferred_element_type=out)  17.5 us
    dot_general x3, matrix products, dot_t(): lax.dot_general(a, b, (((1,), (1,)), ((), ())), preferred_element_type=out)  16 us
  transfers between devices with their start and end apart: 14, of which 8 were waited for; matrix products, arithmetic and copies ran while one was open for 12% of the time, Pallas kernels for 0%

profile of v1, /device:TPU:1, one launch (start us, length us, event | category | flops | bytes accessed | tf_op | source)
XLA Modules:
  0.0 534.1 jit_solution(1895269349851931547)
XLA Ops:
  13.0 38.2 %all_to_all.34 = bf16[64,3,4096]{2,1,0:T(4,128)(2,1)} all-to-all(bf16[64,3,4096]{2,1,0:T(4,128)(2,1)} %reshape.299), channel_id=1, replica_groups=mesh['seq'=4,'zlo'=2,'y'=4,'x'=4,'core'=2] {'zlo','y','x','core'}, dimensions={0} | all-to-all | bytes 3145728 | tf_op jit(solution)/shard_map/all_to_all | solution.py:61
  51.2 4.3 stack.53
  55.4 7.6 %all-to-all-start.2 = ((bf16[8,128,4096]{2,1,0:T(8,128)(2,1)}), bf16[8,128,4096]{2,1,0:T(8,128)(2,1)}, u32[]{:S(2)}, u32[]{:S(2)}) async-start(bf16[8,128,4096]{2,1,0:T(8,128)(2,1)} %stack.53), calls=%async_computation.2 | async-start | bytes 16777216 | tf_op jit(solution)/shard_map/all_to_all | solution.py:58
  63.2 3.6 collective-permute-start.5
  74.6 169.0 %collective-permute-done = f32[2,128]{1,0:T(2,128)S(1)} collective-permute-done((f32[2,128]{1,0:T(2,128)S(1)}, f32[2,128]{1,0:T(2,128)S(1)}, u32[]{:S(2)}, u32[]{:S(2)}) %collective-permute-start) | collective-permute-done | bytes 1056 | tf_op jit(solution)/shard_map/ppermute | solution.py:32
  243.6 5.0 collective-permute-done.1
  252.7 4.3 reshape.300
  258.2 8.1 %all-to-all-start = ((f32[32,1,24]{2,1,0:T(1,128)}), f32[32,1,24]{2,1,0:T(1,128)S(1)}, u32[]{:S(2)}, u32[]{:S(2)}) async-start(f32[32,1,24]{2,1,0:T(1,128)} %bitcast.17), calls=%async_computation | async-start | bytes 32768 | tf_op jit(solution)/shard_map/all_to_all | solution.py:73
  266.3 12.1 %fusion.1 = bf16[32,24,4096]{2,1,0:T(8,128)(2,1)} fusion(bf16[1024,4096,1]{1,0,2:T(8,128)(2,1)} %bitcast.20, s32[32,24]{1,0:T(8,128)S(1)} %multiply_add_fusion, s32[1024]{0:T(1024)S(1)} %bitcast.99), kind=kOutput, calls=%fused_computation.11 | convolution fusion | flops 6443237376 | bytes 14687232 | tf_op jit(solution)/shard_map/dot_general | solution.py:18
  278.4 7.4 %all-to-all-start.3 = ((bf16[32,24,4096]{2,1,0:T(8,128)(2,1)}), bf16[32,24,4096]{2,1,0:T(8,128)(2,1)}, u32[]{:S(2)}, u32[]{:S(2)}) async-start(bf16[32,24,4096]{2,1,0:T(8,128)(2,1)} %fusion.1), calls=%async_computation.3 | async-start | bytes 12582912 | tf_op jit(solution)/shard_map/all_to_all | solution.py:75
  287.7 71.1 %all-to-all-done.3 = bf16[32,24,4096]{2,1,0:T(8,128)(2,1)} async-done(((bf16[32,24,4096]{2,1,0:T(8,128)(2,1)}), bf16[32,24,4096]{2,1,0:T(8,128)(2,1)}, u32[]{:S(2)}, u32[]{:S(2)}) %all-to-all-start.3) | async-done | bytes 6291488 | tf_op jit(solution)/shard_map/all_to_all | solution.py:75
  358.8 5.6 %fusion.66 = f32[768,192]{0,1:T(8,128)S(1)} fusion(bf16[768,4096]{1,0:T(8,128)(2,1)} %bitcast.21, bf16[1,192,4096]{2,1,0:T(8,128)(2,1)} %param.11), kind=kOutput, calls=%fused_computation.125 | convolution fusion | flops 1207959552 | bytes 8454144 | tf_op jit(solution)/shard_map/dot_general | solution.py:22
  364.4 5.0 fusion.68
  369.4 2.9 fusion.6
  373.2 5.4 %multiply_convert_fusion.1 = (bf16[768,192]{0,1:T(8,128)(2,1)S(1)}, bf16[768,192]{0,1:T(8,128)(2,1)S(1)}, bf16[768]{0:T(1024)(128)(2,1)S(1)}) fusion(f32[768]{0:T(1024)S(1)} %select_reduce_fusion.1, f32[768,384]{0,1:T(8,128)} %fusion.6, bf16[768,4096]{1,0:T(8,128)(2,1)} %all-gather.2.cloned.1.call-done, bf16[1,192,4096]{2,1,0:T(8,128)(2,1)S(1)} %copy-done), kind=kOutput, calls=%fused_computation.40 | convolution fusion | flops 1210465536 | bytes 9638400 | tf_op jit(solution)/shard_map/dot_general | solution.py:22
  389.4 55.1 %all_to_all.35 = bf16[32,24,2176]{2,1,0:T(8,128)(2,1)S(1)} all-to-all(bf16[32,24,2176]{2,1,0:T(8,128)(2,1)S(1)} %bitcast.92), channel_id=1, replica_groups=mesh['seq'=4,'zlo'=2,'y'=4,'x'=4,'core'=2] {'y','x','core'}, dimensions={0} | all-to-all | bytes 6684672 | tf_op jit(solution)/shard_map/all_to_all | solution.py:110
  444.5 5.7 %fusion = bf16[1024,2176]{1,0:T(8,128)(2,1)} fusion(bf16[768,2176]{1,0:T(8,128)(2,1)S(1)} %bitcast.93, s32[1024]{0:T(1024)S(1)} %bitcast.100), kind=kOutput, calls=%fused_computation.10 | convolution fusion | flops 3423338496 | bytes 7802880 | tf_op jit(solution)/shard_map/dot_general | solution.py:18
  450.2 5.8 %reduce-scatter.3.cloned.1.call-done = bf16[192,2048]{1,0:T(8,128)(2,1)} async-done(((bf16[768,2048]{1,0:T(8,128)(2,1)}), bf16[192,2048]{1,0:T(8,128)(2,1)}) %reduce-scatter.3.cloned.1.call-update) | async-done | bytes 786448 | tf_op jit(solution)/shard_map/reduce_scatter | solution.py:104
  456.0 3.3 reshape.303
  459.3 8.1 %all-to-all-start.4 = ((bf16[64,3,2048]{2,1,0:T(4,128)(2,1)}), bf16[64,3,2048]{2,1,0:T(4,128)(2,1)S(1)}, u32[]{:S(2)}, u32[]{:S(2)}) async-start(bf16[64,3,2048]{2,1,0:T(4,128)(2,1)} %reshape.303), calls=%async_computation.5 | async-start | bytes 2097152 | tf_op jit(solution)/shard_map/all_to_all | solution.py:113
  467.4 5.9 %convolution_bitcast_fusion.2 = bf16[1,192,4096]{2,1,0:T(8,128)(2,1)} fusion(bf16[768,192]{0,1:T(8,128)(2,1)S(1)} %fusion.5, bf16[768,4096]{1,0:T(8,128)(2,1)} %bitcast.21), kind=kOutput, calls=%fused_computation.5 | convolution fusion | flops 1207959552 | bytes 8159232 | tf_op jit(solution)/shard_map/dot_general | solution.py:26
  473.3 5.5 %convolution_bitcast_fusion.1 = bf16[1,192,4096]{2,1,0:T(8,128)(2,1)} fusion(bf16[768,192]{0,1:T(8,128)(2,1)S(1)} %copy-done.7, bf16[768,4096]{1,0:T(8,128)(2,1)} %bitcast.21), kind=kOutput, calls=%fused_computation.4 | convolution fusion | flops 1207959552 | bytes 8159232 | tf_op jit(solution)/shard_map/dot_general | solution.py:26
  481.5 13.2 %all-to-all-done.4 = bf16[64,3,2048]{2,1,0:T(4,128)(2,1)S(1)} async-done(((bf16[64,3,2048]{2,1,0:T(4,128)(2,1)}), bf16[64,3,2048]{2,1,0:T(4,128)(2,1)S(1)}, u32[]{:S(2)}, u32[]{:S(2)}) %all-to-all-start.4) | async-done | bytes 786464 | tf_op jit(solution)/shard_map/all_to_all | solution.py:113
  495.8 28.3 %reduce-scatter.5.cloned.1.call-done = bf16[128,2176]{1,0:T(8,128)(2,1)} async-done(((bf16[1024,2176]{1,0:T(8,128)(2,1)}), bf16[128,2176]{1,0:T(8,128)(2,1)}) %reduce-scatter.5.cloned.1.call-update) | async-done | bytes 557072 | tf_op jit(solution)/shard_map/reduce_scatter | solution.py:112
  (93 shorter events, 39.5 us)
Async XLA Ops:
  7.2 366.0 %copy-start = (bf16[1,192,4096]{2,1,0:T(8,128)(2,1)S(1)}, bf16[1,192,4096]{2,1,0:T(8,128)(2,1)}, u32[]{:S(2)}) copy-start(bf16[1,192,4096]{2,1,0:T(8,128)(2,1)} %param.12) | copy-start | bytes 4718596
  13.0 38.2 %copy-start.4 = (bf16[128,4096]{1,0:T(8,128)(2,1)S(1)}, bf16[128,4096]{1,0:T(8,128)(2,1)}, u32[]{:S(2)}) copy-start(bf16[128,4096]{1,0:T(8,128)(2,1)} %param.7) | copy-start | bytes 3145732
  55.4 7.7 %copy-start.9 = (bf16[128,1]{0,1:T(2,128)(2,1)S(1)}, bf16[128,1]{0,1:T(2,128)(2,1)}, u32[]{:S(2)}) copy-start(bf16[128,1]{0,1:T(2,128)(2,1)} %param.9) | copy-start | bytes 772
  55.4 7.7 %copy-start.8 = (s32[128,1]{0,1:T(1,128)S(1)}, s32[128,1]{0,1:T(1,128)}, u32[]{:S(2)}) copy-start(s32[128,1]{0,1:T(1,128)} %param.8) | copy-start | bytes 1540
  55.4 202.8 %all-to-all-start.2 = ((bf16[8,128,4096]{2,1,0:T(8,128)(2,1)}), bf16[8,128,4096]{2,1,0:T(8,128)(2,1)}, u32[]{:S(2)}, u32[]{:S(2)}) async-start(bf16[8,128,4096]{2,1,0:T(8,128)(2,1)} %stack.53), calls=%async_computation.2 | async-start | bytes 16777216 | tf_op jit(solution)/shard_map/all_to_all | solution.py:58
  63.1 310.1 %all-gather.2.cloned.1.call-start = ((), (), s32[]{:S(2)}) async-start(), calls=%async_computation.8 | async-start | bytes 7864320 | tf_op jit(solution)/shard_map/all_gather | solution.py:62
  63.2 188.3 %collective-permute-start.5 = (f32[2,128]{1,0:T(2,128)S(1)}, f32[2,128]{1,0:T(2,128)S(1)}, u32[]{:S(2)}, u32[]{:S(2)}) collective-permute-start(f32[2,128]{1,0:T(2,128)S(1)} %pad_maximum_fusion.2), channel_id=1, source_target_pairs={{0,192},{32,224},{64,0},{96,32},{128,64},{160,96},{192,128},{224,1... | collective-permute-start | bytes 3080 | tf_op jit(solution)/shard_map/ppermute | solution.py:32
  66.8 184.7 %collective-permute-start.4 = (f32[2,128]{1,0:T(2,128)S(1)}, f32[2,128]{1,0:T(2,128)S(1)}, u32[]{:S(2)}, u32[]{:S(2)}) collective-permute-start(f32[2,128]{1,0:T(2,128)S(1)} %pad_maximum_fusion.2), channel_id=1, source_target_pairs={{0,160},{32,192},{64,224},{96,0},{128,32},{160,64},{192,96},{224,1... | collective-permute-start | bytes 3080 | tf_op jit(solution)/shard_map/ppermute | solution.py:32
  68.9 182.6 %collective-permute-start.3 = (f32[2,128]{1,0:T(2,128)S(1)}, f32[2,128]{1,0:T(2,128)S(1)}, u32[]{:S(2)}, u32[]{:S(2)}) collective-permute-start(f32[2,128]{1,0:T(2,128)S(1)} %pad_maximum_fusion.2), channel_id=1, source_target_pairs={{0,128},{32,160},{64,192},{96,224},{128,0},{160,32},{192,64},{224,... | collective-permute-start | bytes 3080 | tf_op jit(solution)/shard_map/ppermute | solution.py:32
  71.4 180.0 %collective-permute-start.2 = (f32[2,128]{1,0:T(2,128)S(1)}, f32[2,128]{1,0:T(2,128)S(1)}, u32[]{:S(2)}, u32[]{:S(2)}) collective-permute-start(f32[2,128]{1,0:T(2,128)S(1)} %pad_maximum_fusion.2), channel_id=1, source_target_pairs={{0,96},{32,128},{64,160},{96,192},{128,224},{160,0},{192,32},{224,... | collective-permute-start | bytes 3080 | tf_op jit(solution)/shard_map/ppermute | solution.py:32
  72.1 171.5 %collective-permute-start = (f32[2,128]{1,0:T(2,128)S(1)}, f32[2,128]{1,0:T(2,128)S(1)}, u32[]{:S(2)}, u32[]{:S(2)}) collective-permute-start(f32[2,128]{1,0:T(2,128)S(1)} %pad_maximum_fusion.2), channel_id=1, source_target_pairs={{0,32},{32,64},{64,96},{96,128},{128,160},{160,192},{192,224},{224... | collective-permute-start | bytes 3080 | tf_op jit(solution)/shard_map/ppermute | solution.py:32
  243.6 5.0 collective-permute-start.1
  248.7 3.5 collective-permute-start.6
  258.2 20.2 %all-to-all-start = ((f32[32,1,24]{2,1,0:T(1,128)}), f32[32,1,24]{2,1,0:T(1,128)S(1)}, u32[]{:S(2)}, u32[]{:S(2)}) async-start(f32[32,1,24]{2,1,0:T(1,128)} %bitcast.17), calls=%async_computation | async-start | bytes 32768 | tf_op jit(solution)/shard_map/all_to_all | solution.py:73
  278.4 80.4 %all-to-all-start.3 = ((bf16[32,24,4096]{2,1,0:T(8,128)(2,1)}), bf16[32,24,4096]{2,1,0:T(8,128)(2,1)}, u32[]{:S(2)}, u32[]{:S(2)}) async-start(bf16[32,24,4096]{2,1,0:T(8,128)(2,1)} %fusion.1), calls=%async_computation.3 | async-start | bytes 12582912 | tf_op jit(solution)/shard_map/all_to_all | solution.py:75
  285.8 170.2 %reduce-scatter.3.cloned.1.call-start = ((), (), s32[]{:S(2)}) async-start(), calls=%async_computation.9 | async-start | bytes 3932160 | tf_op jit(solution)/shard_map/reduce_scatter | solution.py:104
  358.8 5.6 %copy-start.1 = (bf16[1,192,4096]{2,1,0:T(8,128)(2,1)S(1)}, bf16[1,192,4096]{2,1,0:T(8,128)(2,1)}, u32[]{:S(2)}) copy-start(bf16[1,192,4096]{2,1,0:T(8,128)(2,1)} %param.10) | copy-start | bytes 4718596
  383.0 141.1 %reduce-scatter.5.cloned.1.call-start = ((), (), s32[]{:S(2)}) async-start(), calls=%async_computation.10 | async-start | bytes 5013504 | tf_op jit(solution)/shard_map/reduce_scatter | solution.py:112
  384.9 2.8 copy-start.6
  459.3 35.4 %all-to-all-start.4 = ((bf16[64,3,2048]{2,1,0:T(4,128)(2,1)}), bf16[64,3,2048]{2,1,0:T(4,128)(2,1)S(1)}, u32[]{:S(2)}, u32[]{:S(2)}) async-start(bf16[64,3,2048]{2,1,0:T(4,128)(2,1)} %reshape.303), calls=%async_computation.5 | async-start | bytes 2097152 | tf_op jit(solution)/shard_map/all_to_all | solution.py:113
  467.4 5.9 %copy-start.7 = (bf16[768,192]{0,1:T(8,128)(2,1)S(1)}, bf16[768,192]{0,1:T(8,128)(2,1)}, u32[]{:S(2)}) copy-start(bf16[768,192]{0,1:T(8,128)(2,1)} %copy-done.6) | copy-start | bytes 884740
  467.4 11.4 %slice-start = ((s8[6291456]{0:T(1024)(128)(4,1)}), s8[4194304]{0:T(1024)(128)(4,1)S(1)}, s32[]{:S(2)}) async-start(s8[6291456]{0:T(1024)(128)(4,1)} %bitcast.103), calls=%async_computation.11 | async-start | bytes 8388608
  473.3 5.5 %slice-start.1 = ((s8[6291456]{0:T(1024)(128)(4,1)}), s8[2097152]{0:T(1024)(128)(4,1)S(1)}, s32[]{:S(2)}) async-start(s8[6291456]{0:T(1024)(128)(4,1)} %bitcast.103), calls=%async_computation.12 | async-start | bytes 4194304
  473.3 5.5 %copy-start.10 = (f32[768,384]{0,1:T(8,128)S(1)}, f32[768,384]{0,1:T(8,128)}, u32[]{:S(2)}) copy-start(f32[768,384]{0,1:T(8,128)} %fusion.6) | copy-start | bytes 3538948
  (3 other events, 4.0 us)
Sparse Core Ops, SparseCore 0:
  257.2 115.9 all-gather.1
  383.1 72.8 reduce-scatter.2
  458.6 65.4 reduce-scatter.4
